TPU v7x, 32 devices: a whole 2x2x4 slice. The times are simulated.
32 devices in a mesh: tm: 8 (over y, x, core), tile: 4 (over z).
Axes of the slice: x: 2, y: 2, z: 4, core: 2. Of those that a mesh axis runs over, the one named last changes fastest.
Arguments:
- local_inv: bfloat16 [16, 2048, 2048], P('tm', None, 'tile'), as said below
- seed_inv: float32 [8, 2048, 2048], P('tm', None, 'tile'), as said below
- band: float32 [16, 16, 3, 128, 128], P('tm', 'tile'), may hold values from -0.25 to 0.25
- pattern: int32 [16, 16, 3], P('tm', 'tile'), may hold values from 0 to 1, as said below
Outputs:
- sigma_first: float32 [8, 2048, 2048], P('tm', None, 'tile')
- variances: float32 [16, 2048], P('tm', 'tile')
Inputs may be any that keep to these rules, and one draw needn't show every extreme that they name: Every entry is 0 or 1; the middle entry pattern[j, b, 1] is 1; pattern[j, 0, 0] and pattern[j, 15, 2] are 0. `local_inv`: each matrix is symmetric. `seed_inv`: each matrix is symmetric.
All inputs are finite; a program needn't handle non-finite values.
Results may differ from a plain program's by a relative error of at most 0.0003.
Values sent between devices are 32-bit elements; how exact they have to be, the bound alone decides.
A program may use at most 128 MiB of HBM per device.

v0:
```python
import jax
import jax.numpy as jnp
from jax import lax
from jax.sharding import PartitionSpec as P

HIGH = lax.Precision.HIGHEST


def padded_2(value, sides, width):
    for axis, dim in sides:
        size, length = (lax.axis_size(axis), value.shape[dim])
        up = [(i, (i + 1) % size) for i in range(size - 1)]
        down = [(j, i) for i, j in up]
        last = lax.slice_in_dim(value, length - width, length, axis=dim)
        leading = lax.slice_in_dim(value, 0, width, axis=dim)
        before = lax.ppermute(last, axis, up)
        after = lax.ppermute(leading, axis, down)
        value = jnp.concatenate([before, value, after], axis=dim)
    return value


def from_behind(block, axis, distance):
    devices = range(lax.axis_size(axis))
    route = [(i - distance, i) for i in devices if i - distance in devices]
    return lax.ppermute(block, axis, route)


def column_product(field, weff):
    tile_rows = weff.shape[2]
    local_tiles = weff.shape[0]
    row_count = field.shape[0]
    extended = padded_2(field, (("tile", 1),), tile_rows)
    extended = extended.reshape(row_count, local_tiles + 2, tile_rows)
    windows = jnp.stack([extended[:, offset : offset + local_tiles] for offset in range(3)], axis=2)
    product = jnp.einsum("rikc,ikcd->rid", windows, weff, precision=HIGH)
    return product.reshape(row_count, local_tiles * tile_rows)


def left_gathered(product, whole_band):
    tiles = whole_band.shape[0]
    tile_rows = whole_band.shape[2]
    slab_width = product.shape[1]
    spread = product.reshape(tiles, tile_rows, slab_width)
    padded = jnp.pad(spread, ((1, 1), (0, 0), (0, 0)))
    windows = jnp.stack([padded[offset : offset + tiles] for offset in range(3)], axis=1)
    result = jnp.einsum("skcd,skce->sde", whole_band, windows, precision=HIGH)
    return result.reshape(tiles * tile_rows, slab_width)


def per_device(local_inv, seed_inv, band, pattern):
    weff = band * pattern.astype(jnp.float32)[..., None, None]
    incoming = from_behind(seed_inv, "tm", -1)[0]
    whole_band = lax.all_gather(weff, "tile", axis=1, tiled=True)

    def apply_step(field, index):
        product = column_product(field, weff[index])
        return local_inv[index].astype(jnp.float32) + left_gathered(product, whole_band[index])

    sigma_odd = apply_step(incoming, 1)
    sigma_even = apply_step(sigma_odd, 0)
    slab_width = sigma_even.shape[1]
    start = lax.axis_index("tile") * slab_width
    diag_even = jnp.diagonal(lax.dynamic_slice_in_dim(sigma_even, start, slab_width, 0))
    diag_odd = jnp.diagonal(lax.dynamic_slice_in_dim(sigma_odd, start, slab_width, 0))
    variances = jnp.stack([diag_even, diag_odd])
    return (sigma_even[None], variances)


def solution(mesh):
    placed = (
        P("tm", None, "tile"),
        P("tm", None, "tile"),
        P("tm", "tile", None, None, None),
        P("tm", "tile", None),
    )
    return jax.shard_map(
        per_device,
        mesh=mesh,
        in_specs=placed,
        out_specs=(P("tm", None, "tile"), P("tm", "tile")),
        check_vma=False,
    )
```

profile of v0, /device:TPU:5, one launch (start us, length us, event | category | flops | bytes accessed | tf_op | source)
XLA Modules:
  0.0 359.6 jit_solution(8053937794287284997)
XLA Ops:
  7.2 0.0 all-gather.2.cloned.1.call-start
  7.2 1.9 copy.19
  9.1 0.7 convert_element_type.22
  9.8 0.1 copy.18
  9.9 1.3 broadcast_multiply_fusion
  11.2 0.0 all-gather.2.cloned.1.call-update
  11.2 5.3 %copy.20 = f32[1,2048,512]{1,2,0:T(8,128)} copy(f32[1,2048,512]{2,1,0:T(8,128)} %param.5) | data formatting | bytes 8388608 | tf_op args[1]
  16.6 2.6 collective-permute-start
  19.2 47.9 %collective-permute-done = f32[1,2048,512]{1,2,0:T(8,128)S(1)} collective-permute-done((f32[1,2048,512]{1,2,0:T(8,128)}, f32[1,2048,512]{1,2,0:T(8,128)S(1)}, u32[]{:S(2)}, u32[]{:S(2)}) %collective-permute-start) | collective-permute-done | bytes 4194336 | tf_op jit(solution)/shard_map/ppermute | solution.py:25
  67.0 0.2 fusion.35
  67.3 2.9 collective-permute-start.1
  70.1 1.3 collective-permute-start.2
  71.4 44.2 %collective-permute-done.1 = f32[2048,128]{0,1:T(8,128)S(1)} collective-permute-done((f32[2048,128]{0,1:T(8,128)S(1)}, f32[2048,128]{0,1:T(8,128)S(1)}, u32[]{:S(2)}, u32[]{:S(2)}) %collective-permute-start.1) | collective-permute-done | bytes 1048608 | tf_op jit(solution)/shard_map/ppermute | solution.py:16
  115.6 28.1 %collective-permute-done.2 = f32[2048,128]{0,1:T(8,128)S(1)} collective-permute-done((f32[2048,128]{0,1:T(8,128)S(1)}, f32[2048,128]{0,1:T(8,128)S(1)}, u32[]{:S(2)}, u32[]{:S(2)}) %collective-permute-start.2) | collective-permute-done | bytes 1048608 | tf_op jit(solution)/shard_map/ppermute | solution.py:17
  143.7 0.4 pad_maximum_fusion
  144.2 5.0 %fusion.33 = (f32[2048,4,128]{0,2,1:T(8,128)}, f32[2048,4,128]{0,2,1:T(8,128)}, f32[2048,4,128]{0,2,1:T(8,128)}) fusion(f32[2048,6,128]{0,2,1:T(8,128)S(1)} %bitcast.84), kind=kLoop, calls=%fused_computation.53 | loop fusion | bytes 25165824 | tf_op jit(solution)/shard_map/slice | solution.py:34
  149.1 5.3 %copy.38 = f32[2048,4,128]{2,0,1:T(8,128)} copy(f32[2048,4,128]{0,2,1:T(8,128)} %get-tuple-element.5) | data formatting | bytes 8388608
  154.5 5.3 %copy.39 = f32[2048,4,128]{2,0,1:T(8,128)} copy(f32[2048,4,128]{0,2,1:T(8,128)} %get-tuple-element.6) | data formatting | bytes 8388608
  159.8 0.0 copy-start.2
  159.8 5.5 %copy.40 = f32[2048,4,128]{2,0,1:T(8,128)} copy(f32[2048,4,128]{0,2,1:T(8,128)} %get-tuple-element.7) | data formatting | bytes 8388608
  165.3 0.0 copy-done.2
  165.3 15.8 %fusion = f32[4,128,2048,1]{2,1,3,0:T(8,128)S(1)} fusion(f32[2048,4,1,128]{3,0,2,1:T(8,128)} %bitcast.98, f32[2048,4,1,128]{3,0,2,1:T(8,128)} %bitcast.95, f32[2048,4,1,128]{3,0,2,1:T(8,128)} %bitcast.93, f32[2,4,3,128,128]{3,4,2,1,0:T(8,128)S(1)} %copy-done.2), kind=kOutput, calls=%fused_computation.2 | convolution fusion | flops 4838129664 | bytes 17563648 | tf_op jit(solution)/shard_map/rikc,ikcd->rid/dot_general | solution.py:35
  181.0 2.9 copy.44
  184.0 5.4 %copy.24 = f32[16,128,512]{2,1,0:T(8,128)} copy(f32[16,128,512]{1,0,2:T(8,128)} %bitcast.88) | data formatting | bytes 8388608 | tf_op jit(solution)/shard_map/reshape;reshape | solution.py:43
  189.3 5.3 %copy.26 = f32[16,1,128,512]{3,2,1,0:T(8,128)} copy(f32[16,1,128,512]{2,0,3,1:T(8,128)} %bitcast.89) | data formatting | bytes 8388608 | tf_op jit(solution)/shard_map/stack | solution.py:45
  194.6 8.2 %fusion.24 = (f32[16,1,128,512]{3,2,1,0:T(8,128)}, f32[16,1,128,512]{3,2,1,0:T(8,128)}) fusion(f32[16,128,512]{2,1,0:T(8,128)} %copy.24), kind=kLoop, calls=%fused_computation.34 | loop fusion | bytes 12582912 | tf_op jit(solution)/shard_map/stack | solution.py:45
  202.8 0.0 all-gather.2.cloned.1.call-done
  202.8 0.0 copy-start.3
  202.8 11.9 %fusion.6 = f32[16,128,512,1]{2,1,3,0:T(8,128)S(1)} fusion(f32[16,1,128,512]{3,2,1,0:T(8,128)} %get-tuple-element.13, f32[16,1,128,512]{3,2,1,0:T(8,128)} %copy.26, f32[16,1,128,512]{3,2,1,0:T(8,128)} %get-tuple-element.12, f32[2,16,3,128,128]{3,4,2,1,0:T(8,128)} %all-gather.2.cloned.1.call-done), kind=kOutput, calls=%fused_computation.8 | convolution fusion | flops 4838129664 | bytes 19922944 | tf_op jit(solution)/shard_map/skcd,skce->sde/dot_general | solution.py:46
  214.8 0.0 copy-done.3
  214.8 0.7 bitcast_add_fusion
  215.4 0.0 copy-start
  215.5 2.0 copy-done
  217.5 1.4 fusion.34
  218.9 5.9 %collective-permute-start.3 = (f32[2048,128]{1,0:T(8,128)}, f32[2048,128]{1,0:T(8,128)}, u32[]{:S(2)}, u32[]{:S(2)}) collective-permute-start(f32[2048,128]{1,0:T(8,128)} %get-tuple-element.10), channel_id=1, source_target_pairs={{0,1},{1,2},{2,3},{4,5},{5,6},{6,7},{8,9},{9,10},{10,11},{12,13},{... | collective-permute-start | bytes 3145736 | tf_op jit(solution)/shard_map/ppermute | solution.py:16
  224.9 1.3 collective-permute-start.4
  226.2 4.2 %convert_bitcast_fusion = f32[2048,512]{1,0:T(8,128)} fusion(bf16[2,2048,512]{2,1,0:T(8,128)(2,1)} %param.4), kind=kLoop, calls=%fused_computation.28 | loop fusion | flops 1048576 | bytes 6291456 | tf_op jit(solution)/shard_map/convert_element_type | solution.py:57
  230.4 1.3 constant_dynamic-slice_fusion
  231.7 4.5 %gather_fusion.1 = f32[512]{0:T(512)S(1)} fusion(f32[512,512]{1,0:T(8,128)S(1)} %constant_dynamic-slice_fusion, s32[512]{0:T(512)S(1)} %bitcast.82), kind=kCustom, calls=%fused_computation.1 | custom fusion | bytes 8192 | tf_op jit(solution)/shard_map/jit(diagonal)/cond/branch_0_fun/gather | solution.py:64
  236.2 10.2 %collective-permute-done.3 = f32[2048,128]{1,0:T(8,128)} collective-permute-done((f32[2048,128]{1,0:T(8,128)}, f32[2048,128]{1,0:T(8,128)}, u32[]{:S(2)}, u32[]{:S(2)}) %collective-permute-start.3) | collective-permute-done | bytes 1048608 | tf_op jit(solution)/shard_map/ppermute | solution.py:16
  246.4 4.8 %collective-permute-done.4 = f32[2048,128]{1,0:T(8,128)} collective-permute-done((f32[2048,128]{1,0:T(8,128)}, f32[2048,128]{1,0:T(8,128)}, u32[]{:S(2)}, u32[]{:S(2)}) %collective-permute-start.4) | collective-permute-done | bytes 1048608 | tf_op jit(solution)/shard_map/ppermute | solution.py:17
  251.2 5.9 %pad_maximum_fusion.1 = f32[2048,768]{1,0:T(8,128)} fusion(f32[2048,128]{1,0:T(8,128)} %collective-permute-done.4, f32[2048,512]{1,0:T(8,128)} %copy-done, f32[2048,128]{1,0:T(8,128)} %collective-permute-done.3), kind=kLoop, calls=%fused_computation.27 | loop fusion | flops 3145728 | bytes 12582912 | tf_op jit(solution)/shard_map/concatenate | solution.py:18
  257.1 6.5 %copy.27 = f32[2048,768]{0,1:T(8,128)} copy(f32[2048,768]{1,0:T(8,128)} %pad_maximum_fusion.1) | data formatting | bytes 12582912 | tf_op jit(solution)/shard_map/concatenate | solution.py:18
  263.6 9.8 %fusion.32 = (f32[2048,4,128]{0,2,1:T(8,128)}, f32[2048,4,128]{0,2,1:T(8,128)}, f32[2048,4,128]{0,2,1:T(8,128)}) fusion(f32[2048,6,128]{0,2,1:T(8,128)} %bitcast.85), kind=kLoop, calls=%fused_computation.52 | loop fusion | bytes 25165824 | tf_op jit(solution)/shard_map/slice | solution.py:34
  273.5 5.3 %copy.41 = f32[2048,4,128]{2,0,1:T(8,128)} copy(f32[2048,4,128]{0,2,1:T(8,128)} %get-tuple-element.2) | data formatting | bytes 8388608
  278.8 5.3 %copy.42 = f32[2048,4,128]{2,0,1:T(8,128)} copy(f32[2048,4,128]{0,2,1:T(8,128)} %get-tuple-element.3) | data formatting | bytes 8388608
  284.2 5.3 %copy.43 = f32[2048,4,128]{2,0,1:T(8,128)} copy(f32[2048,4,128]{0,2,1:T(8,128)} %get-tuple-element.4) | data formatting | bytes 8388608
  289.5 15.8 %fusion.12 = f32[4,128,2048,1]{2,1,3,0:T(8,128)S(1)} fusion(f32[2048,4,1,128]{3,0,2,1:T(8,128)} %bitcast.96, f32[2048,4,1,128]{3,0,2,1:T(8,128)} %bitcast.94, f32[2048,4,1,128]{3,0,2,1:T(8,128)} %bitcast.92, f32[2,4,3,128,128]{3,4,2,1,0:T(8,128)S(1)} %copy-done.2), kind=kOutput, calls=%fused_computation.14 | convolution fusion | flops 4838129664 | bytes 17563648 | tf_op jit(solution)/shard_map/rikc,ikcd->rid/dot_general | solution.py:35
  305.3 2.9 copy.46
  308.2 5.4 %copy.31 = f32[16,128,512]{2,1,0:T(8,128)} copy(f32[16,128,512]{1,0,2:T(8,128)} %bitcast.86) | data formatting | bytes 8388608 | tf_op jit(solution)/shard_map/reshape;reshape | solution.py:43
  313.5 8.1 %fusion.26 = (f32[16,1,128,512]{3,2,1,0:T(8,128)}, f32[16,1,128,512]{3,2,1,0:T(8,128)}) fusion(f32[16,128,512]{2,1,0:T(8,128)} %copy.31), kind=kLoop, calls=%fused_computation.36 | loop fusion | bytes 12582912 | tf_op jit(solution)/shard_map/stack | solution.py:45
  321.6 5.4 %copy.33 = f32[16,1,128,512]{3,2,1,0:T(8,128)} copy(f32[16,1,128,512]{2,0,3,1:T(8,128)} %bitcast.87) | data formatting | bytes 8388608 | tf_op jit(solution)/shard_map/stack | solution.py:45
  327.0 11.6 %fusion.18 = f32[16,128,512,1]{2,1,3,0:T(8,128)S(1)} fusion(f32[16,1,128,512]{3,2,1,0:T(8,128)} %get-tuple-element.9, f32[16,1,128,512]{3,2,1,0:T(8,128)} %copy.33, f32[16,1,128,512]{3,2,1,0:T(8,128)} %get-tuple-element.8, f32[2,16,3,128,128]{3,4,2,1,0:T(8,128)} %all-gather.2.cloned.1.call-done), kind=kOutput, calls=%fused_computation.20 | convolution fusion | flops 4838129664 | bytes 19922944 | tf_op jit(solution)/shard_map/skcd,skce->sde/dot_general | solution.py:46
  338.6 0.0 copy-start.1
  338.6 2.0 copy-done.1
  340.6 1.4 dynamic-slice_add_fusion
  342.1 4.5 %gather_fusion = f32[512]{0:T(512)S(1)} fusion(f32[512,512]{1,0:T(8,128)S(1)} %dynamic-slice_add_fusion, s32[512]{0:T(512)S(1)} %bitcast.83), kind=kCustom, calls=%fused_computation | custom fusion | bytes 8192 | tf_op jit(solution)/shard_map/jit(diagonal)/cond/branch_0_fun/gather | solution.py:63
  346.6 5.5 %convert_add_fusion = f32[1,2048,512]{2,1,0:T(8,128)} fusion(f32[1,2048,512]{2,1,0:T(8,128)} %bitcast.91, bf16[2,2048,512]{2,1,0:T(8,128)(2,1)} %param.4), kind=kLoop, calls=%fused_computation.29 | loop fusion | flops 2097152 | bytes 10485760 | tf_op jit(solution)/shard_map/add | solution.py:57
  352.2 0.6 pad_maximum_fusion.2
  (1 shorter events, 0.0 us)
Async XLA Ops:
  7.2 195.7 %all-gather.2.cloned.1.call-start = ((), (), s32[]{:S(2)}) async-start(), calls=%async_computation | async-start | bytes 7864320 | tf_op jit(solution)/shard_map/all_gather | solution.py:53
  16.6 50.5 %collective-permute-start = (f32[1,2048,512]{1,2,0:T(8,128)}, f32[1,2048,512]{1,2,0:T(8,128)S(1)}, u32[]{:S(2)}, u32[]{:S(2)}) collective-permute-start(f32[1,2048,512]{1,2,0:T(8,128)} %copy.20), channel_id=1, source_target_pairs={{4,0},{8,4},{12,8},{16,12},{20,16},{24,20},{28,24},{5,1},{9,5},{13... | collective-permute-start | bytes 12582920 | tf_op jit(solution)/shard_map/ppermute | solution.py:25
  67.3 48.3 %collective-permute-start.1 = (f32[2048,128]{0,1:T(8,128)S(1)}, f32[2048,128]{0,1:T(8,128)S(1)}, u32[]{:S(2)}, u32[]{:S(2)}) collective-permute-start(f32[2048,128]{0,1:T(8,128)S(1)} %get-tuple-element.14), channel_id=1, source_target_pairs={{0,1},{1,2},{2,3},{4,5},{5,6},{6,7},{8,9},{9,10},{10,11},{12,13},{... | collective-permute-start | bytes 3145736 | tf_op jit(solution)/shard_map/ppermute | solution.py:16
  70.1 73.6 %collective-permute-start.2 = (f32[2048,128]{0,1:T(8,128)S(1)}, f32[2048,128]{0,1:T(8,128)S(1)}, u32[]{:S(2)}, u32[]{:S(2)}) collective-permute-start(f32[2048,128]{0,1:T(8,128)S(1)} %get-tuple-element.15), channel_id=1, source_target_pairs={{1,0},{2,1},{3,2},{5,4},{6,5},{7,6},{9,8},{10,9},{11,10},{13,12},{... | collective-permute-start | bytes 3145736 | tf_op jit(solution)/shard_map/ppermute | solution.py:17
  159.8 5.5 %copy-start.2 = (f32[2,4,3,128,128]{3,4,2,1,0:T(8,128)S(1)}, f32[2,4,3,128,128]{3,4,2,1,0:T(8,128)}, u32[]{:S(2)}) copy-start(f32[2,4,3,128,128]{3,4,2,1,0:T(8,128)} %broadcast_multiply_fusion) | copy-start | bytes 4718596
  202.8 12.0 %copy-start.3 = (bf16[2,2048,512]{2,1,0:T(8,128)(2,1)S(1)}, bf16[2,2048,512]{2,1,0:T(8,128)(2,1)}, u32[]{:S(2)}) copy-start(bf16[2,2048,512]{2,1,0:T(8,128)(2,1)} %param.4) | copy-start | bytes 12582916
  215.4 2.0 copy-start
  218.9 27.5 %collective-permute-start.3 = (f32[2048,128]{1,0:T(8,128)}, f32[2048,128]{1,0:T(8,128)}, u32[]{:S(2)}, u32[]{:S(2)}) collective-permute-start(f32[2048,128]{1,0:T(8,128)} %get-tuple-element.10), channel_id=1, source_target_pairs={{0,1},{1,2},{2,3},{4,5},{5,6},{6,7},{8,9},{9,10},{10,11},{12,13},{... | collective-permute-start | bytes 3145736 | tf_op jit(solution)/shard_map/ppermute | solution.py:16
  224.9 26.4 %collective-permute-start.4 = (f32[2048,128]{1,0:T(8,128)}, f32[2048,128]{1,0:T(8,128)}, u32[]{:S(2)}, u32[]{:S(2)}) collective-permute-start(f32[2048,128]{1,0:T(8,128)} %get-tuple-element.11), channel_id=1, source_target_pairs={{1,0},{2,1},{3,2},{5,4},{6,5},{7,6},{9,8},{10,9},{11,10},{13,12},{... | collective-permute-start | bytes 3145736 | tf_op jit(solution)/shard_map/ppermute | solution.py:17
  338.6 2.0 copy-start.1
Sparse Core Ops, SparseCore 0:
  11.3 138.9 all-gather.1
where the time goes:
time: 362 us; the launch traced here: 360 us
  waiting for transfers between devices  135 us (37%)
  local copies, waits for them, and re-layouts  120 us (33%)
  matrix products  55.1 us (15%)
  other arithmetic  20.8 us (6%)
  between operations  14.2 us (4%)
  starting transfers between devices  14 us (4%)
    ppermute x2, waiting for transfers between devices, padded_2(): before = lax.ppermute(last, axis, up)  54.4 us
    unnamed x18, local copies, waits for them, and re-layouts  49.3 us
    ppermute x1, waiting for transfers between devices, from_behind(): return lax.ppermute(block, axis, route)  47.9 us
    ppermute x2, waiting for transfers between devices, padded_2(): after = lax.ppermute(leading, axis, down)  32.9 us
    dot_general x2, matrix products, column_product(): product = jnp.einsum('rikc,ikcd->rid', windows, weff, precision=HIGH)  31.5 us
    another operation x4, local copies, waits for them, and re-layouts, left_gathered(): jnp.stack([padded[offset:offset + tiles] for offset in range(3)], axis=1)  26.9 us
    dot_general x2, matrix products, left_gathered(): result = jnp.einsum('skcd,skce->sde', whole_band, windows, precision=HIGH)  23.6 us
    slice x2, local copies, waits for them, and re-layouts, column_product(): extended[:, offset:offset + local_tiles]  14.8 us
  transfers between devices with their start and end apart: 6, of which 5 were waited for; matrix products, arithmetic and copies ran while one was open for 21% of the time, Pallas kernels for 0%

commit v1 on v0

v1 whole, which is shorter than its diff:
```python
import functools

import jax
import jax.numpy as jnp
from jax import lax
from jax.experimental import pallas as pl
from jax.experimental.pallas import tpu as pltpu
from jax.sharding import PartitionSpec as P

F32 = jnp.float32
BF16 = jnp.bfloat16
MESH = pl.DeviceIdType.MESH


def split(value):
    high = value.astype(BF16)
    return high, (value - high.astype(F32)).astype(BF16)


def dot(a, b):
    return lax.dot_general(a, b, (((1,), (0,)), ((), ())), preferred_element_type=F32)


def split_dot(a_high, a_low, b_high, b_low):
    return dot(a_high, b_high) + (dot(a_high, b_low) + dot(a_low, b_high))


def kernel(parts, ranks, local_ref, seed_ref, weff_ref, out_ref, var_ref,
           nxt, odd, wbuf, m_high, m_low, loc, wc_high, wc_low, wt_high, wt_low,
           wsend, wrecv, nsend, nrecv, hsend, hrecv, lsem):
    p, t = lax.axis_index("tm"), lax.axis_index("tile")
    rows, width = seed_ref.shape[1], seed_ref.shape[2]
    tiles, tr = wbuf.shape[1], wbuf.shape[3]
    lt = width // tr
    g = 2 if lt % 2 == 0 else 1
    span = (g + 2) * tr
    inner = pl.ds(tr, width)
    left_halo, right_halo = pl.ds(0, tr), pl.ds(tr + width, tr)
    has_right, has_left = t < ranks - 1, t > 0
    has_next = p < parts - 1

    barrier = pltpu.get_barrier_semaphore()
    around = [(a, b) for a in (-1, 0, 1) for b in (-1, 0, 1) if (a, b) != (0, 0)]

    def present(a, b):
        return (p + a >= 0) & (p + a < parts) & (t + b >= 0) & (t + b < ranks)

    for a, b in around:
        @pl.when(present(a, b))
        def _(a=a, b=b):
            pl.semaphore_signal(barrier, inc=1, device_id={"tm": p + a, "tile": t + b}, device_id_type=MESH)
    near_tm = 1 + jnp.where(p > 0, 1, 0) + jnp.where(p < parts - 1, 1, 0)
    near_tile = 1 + jnp.where(t > 0, 1, 0) + jnp.where(t < ranks - 1, 1, 0)
    pl.semaphore_wait(barrier, near_tm * near_tile - 1)

    def toward(d):
        return (1, has_right) if d == 0 else (-1, has_left)

    def own_w(j, d):
        step, _ = toward(d)
        return pltpu.make_async_remote_copy(
            src_ref=weff_ref.at[j], dst_ref=wbuf.at[j, pl.ds(t * lt, lt)],
            send_sem=wsend.at[j, d, 0], recv_sem=wrecv.at[j, d, 1],
            device_id={"tile": t + step}, device_id_type=MESH)

    def relay_w(j, d, k):
        step, _ = toward(d)
        part = wbuf.at[j, pl.ds((t - step * k) * lt, lt)]
        return pltpu.make_async_remote_copy(
            src_ref=part, dst_ref=part,
            send_sem=wsend.at[j, d, k], recv_sem=wrecv.at[j, d, k + 1],
            device_id={"tile": t + step}, device_id_type=MESH)

    def arriving_w(j, d, k):
        step, _ = toward(d)
        part = wbuf.at[j, pl.ds((t - step * k) * lt, lt)]
        return pltpu.make_async_remote_copy(
            src_ref=part, dst_ref=part,
            send_sem=wsend.at[j, d, k], recv_sem=wrecv.at[j, d, k],
            device_id={"tile": t - step}, device_id_type=MESH)

    def comes(d, k):
        return t - k >= 0 if d == 0 else t + k < ranks

    def start_own(j):
        for d in (1, 0):
            @pl.when(toward(d)[1])
            def _(d=d):
                own_w(j, d).start()

    def receive(j, k):
        for d in (1, 0):
            @pl.when(comes(d, k))
            def _(d=d):
                arriving_w(j, d, k).wait_recv()

                @pl.when(toward(d)[1])
                def _():
                    relay_w(j, d, k).start()

    def seed_copy(index):
        if index == 0:
            src, dst, target = seed_ref.at[0], nxt.at[:, inner], t
        elif index == 1:
            src, dst, target = seed_ref.at[0, :, pl.ds(width - tr, tr)], nxt.at[:, left_halo], t + 1
        else:
            src, dst, target = seed_ref.at[0, :, pl.ds(0, tr)], nxt.at[:, right_halo], t - 1
        return pltpu.make_async_remote_copy(
            src_ref=src, dst_ref=dst, send_sem=nsend.at[index], recv_sem=nrecv.at[index],
            device_id={"tm": p - 1, "tile": target}, device_id_type=MESH)

    seed_sent = ((0, p > 0), (1, (p > 0) & has_right), (2, (p > 0) & has_left))
    seed_received = ((0, has_next), (1, has_next & has_left), (2, has_next & has_right))

    def halo_copy(d):
        if d == 0:
            src, dst, target = odd.at[:, pl.ds(width, tr)], odd.at[:, left_halo], t + 1
        else:
            src, dst, target = odd.at[:, pl.ds(tr, tr)], odd.at[:, right_halo], t - 1
        return pltpu.make_async_remote_copy(
            src_ref=src, dst_ref=dst, send_sem=hsend.at[d], recv_sem=hrecv.at[d],
            device_id={"tile": target}, device_id_type=MESH)

    start_own(1)
    for index, does in seed_sent:
        @pl.when(does)
        def _(index=index):
            seed_copy(index).start()
    own_local = [pltpu.make_async_copy(weff_ref.at[j], wbuf.at[j, pl.ds(t * lt, lt)], lsem.at[j]) for j in (0, 1)]
    locals_in = pltpu.make_async_copy(local_ref, loc, lsem.at[2])
    for copy in own_local + [locals_in]:
        copy.start()

    zero_halo = jnp.zeros((rows, tr), F32)
    for missing, place in ((t == 0, left_halo), (t == ranks - 1, right_halo)):
        @pl.when(missing)
        def _(place=place):
            odd[:, place] = zero_halo

            @pl.when(has_next)
            def _():
                nxt[:, place] = zero_halo

    @pl.when(p == parts - 1)
    def _():
        nxt[...] = jnp.zeros_like(nxt)

    for ref in (m_high, m_low):
        ref[pl.ds(0, tr), :] = jnp.zeros((tr, width), BF16)
        ref[pl.ds(tr + rows, tr), :] = jnp.zeros((tr, width), BF16)
    for ref in (wc_high, wc_low, wt_high, wt_low):
        ref[...] = jnp.zeros_like(ref)
    for copy in own_local:
        copy.wait()

    chunk = 256

    def column_product(field, j):
        for i in range(lt // g):
            for c in range(g):
                for k in range(3):
                    high, low = split(wbuf[j, t * lt + i * g + c, k])
                    at = (i, pl.ds((c + k) * tr, tr), pl.ds(c * tr, tr))
                    wc_high[at] = high
                    wc_low[at] = low

        @pl.loop(0, rows // chunk)
        def _(r):
            start = pl.multiple_of(r * chunk, chunk)
            for i in range(lt // g):
                high, low = split(field[pl.ds(start, chunk), pl.ds(i * g * tr, span)])
                value = split_dot(high, low, wc_high[i], wc_low[i])
                at = (pl.ds(pl.multiple_of(start + tr, tr), chunk), pl.ds(i * g * tr, g * tr))
                high, low = split(value)
                m_high[at] = high
                m_low[at] = low

    def left_rows(j, owner, target, columns):
        @pl.loop(0, lt // g)
        def _(i):
            first = owner * lt + i * g
            for c in range(g):
                for k in range(3):
                    high, low = split(wbuf[j, first + c, k].T)
                    at = (pl.ds(c * tr, tr), pl.ds((c + k) * tr, tr))
                    wt_high[at] = high
                    wt_low[at] = low
            start = pl.multiple_of(first * tr, tr)
            source = pl.ds(start, span)
            value = split_dot(wt_high[...], wt_low[...], m_high[source, :], m_low[source, :])
            place = pl.ds(start, g * tr)
            target[place, columns] = loc[j, place, :].astype(F32) + value

    def left_round(j, k, target, columns):
        for d in (1, 0):
            @pl.when(comes(d, k))
            def _(d=d):
                left_rows(j, t - k if d == 0 else t + k, target, columns)

    def diagonal(index, field, offset):
        eye = lax.broadcasted_iota(jnp.int32, (tr, tr), 0) == lax.broadcasted_iota(jnp.int32, (tr, tr), 1)
        for c in range(lt):
            tile = field[pl.ds(pl.multiple_of(t * width + c * tr, tr), tr), pl.ds(offset + c * tr, tr)]
            var_ref[pl.ds(index, 1), pl.ds(c * tr, tr)] = jnp.sum(jnp.where(eye, tile, 0.0), axis=0, keepdims=True)

    receive(1, 1)
    start_own(0)
    for index, does in seed_received:
        @pl.when(does)
        def _(index=index):
            seed_copy(index).wait_recv()
    column_product(nxt, 1)
    locals_in.wait()
    left_rows(1, t, odd, inner)
    left_round(1, 1, odd, inner)

    @pl.loop(2, ranks)
    def _(k):
        receive(1, k)
        left_round(1, k, odd, inner)

    diagonal(1, odd, tr)
    for d, does in ((1, has_left), (0, has_right)):
        @pl.when(does)
        def _(d=d):
            halo_copy(d).start()

    @pl.loop(1, ranks - 1)
    def _(k):
        receive(0, k)

    for d, does in ((0, has_left), (1, has_right)):
        @pl.when(does)
        def _(d=d):
            halo_copy(d).wait_recv()
    column_product(odd, 0)
    everything = pl.ds(0, width)
    left_rows(0, t, out_ref, everything)

    @pl.loop(1, ranks - 1)
    def _(k):
        left_round(0, k, out_ref, everything)

    receive(0, ranks - 1)
    left_round(0, ranks - 1, out_ref, everything)
    diagonal(0, out_ref, 0)

    for j in (1, 0):
        for d in (1, 0):
            @pl.when(toward(d)[1])
            def _(j=j, d=d):
                own_w(j, d).wait_send()

                @pl.loop(1, ranks - 1)
                def _(k):
                    @pl.when(comes(d, k))
                    def _():
                        relay_w(j, d, k).wait_send()
    for index, does in seed_sent:
        @pl.when(does)
        def _(index=index):
            seed_copy(index).wait_send()
    for d, does in ((0, has_right), (1, has_left)):
        @pl.when(does)
        def _(d=d):
            halo_copy(d).wait_send()


def per_device(parts, ranks, local_inv, seed_inv, band, pattern):
    weff = band * pattern.astype(F32)[..., None, None]
    rows, width = seed_inv.shape[1:]
    lt, tr = band.shape[1], band.shape[3]
    tiles = rows // tr
    g = 2 if lt % 2 == 0 else 1
    span = (g + 2) * tr
    dma = pltpu.SemaphoreType.DMA
    out, var = pl.pallas_call(
        functools.partial(kernel, parts, ranks),
        out_shape=(jax.ShapeDtypeStruct((rows, width), F32), jax.ShapeDtypeStruct((2, width), F32)),
        in_specs=[pl.BlockSpec(memory_space=pl.ANY)] * 3,
        out_specs=(pl.BlockSpec(memory_space=pltpu.VMEM), pl.BlockSpec(memory_space=pltpu.VMEM)),
        scratch_shapes=[
            pltpu.VMEM((rows, width + 2 * tr), F32),
            pltpu.VMEM((rows, width + 2 * tr), F32),
            pltpu.VMEM((2, tiles, 3, tr, tr), F32),
            pltpu.VMEM((rows + 2 * tr, width), BF16),
            pltpu.VMEM((rows + 2 * tr, width), BF16),
            pltpu.VMEM((2, rows, width), BF16),
            pltpu.VMEM((lt // g, span, g * tr), BF16),
            pltpu.VMEM((lt // g, span, g * tr), BF16),
            pltpu.VMEM((g * tr, span), BF16),
            pltpu.VMEM((g * tr, span), BF16),
            dma((2, 2, ranks + 1)),
            dma((2, 2, ranks + 1)),
            dma((3,)),
            dma((3,)),
            dma((2,)),
            dma((2,)),
            dma((3,)),
        ],
        compiler_params=pltpu.CompilerParams(
            collective_id=0, has_side_effects=True, vmem_limit_bytes=60 * 1024 * 1024
        ),
    )(local_inv, seed_inv, weff)
    return out[None], var


def solution(mesh):
    placed = (
        P("tm", None, "tile"),
        P("tm", None, "tile"),
        P("tm", "tile", None, None, None),
        P("tm", "tile", None),
    )
    return jax.shard_map(
        functools.partial(per_device, mesh.shape["tm"], mesh.shape["tile"]),
        mesh=mesh,
        in_specs=placed,
        out_specs=(P("tm", None, "tile"), P("tm", "tile")),
        check_vma=False,
    )
```

time: 362 us -> 165 us (0.46)
  Pallas kernels: 0 us -> 155 us
  waiting for transfers between devices: 135 us -> 0 us
  local copies, waits for them, and re-layouts: 120 us -> 5.34 us
  matrix products: 55.1 us -> 0 us
  other arithmetic: 20.8 us -> 3.41 us
  starting transfers between devices: 14 us -> 0 us
  between operations: 14.2 us -> 0.65 us
    pallas_call x0 -> x1, Pallas kernels: none -> 155 us  [per_device(): pl.pallas_call(functools.partial(kernel, parts, ranks), out_shape=(jax.Sh...]
    ppermute x5 -> x0, waiting for transfers between devices: 135 us -> none  [the longest x2 54.4 us: padded_2(): before = lax.ppermute(last, axis, up)]
    dot_general x4 -> x0, matrix products: 55.1 us -> none  [the longest x2 31.5 us: column_product(): product = jnp.einsum('rikc,ikcd->rid', windows, weff, precision=HIGH)]
    unnamed x18 -> x4, local copies, waits for them, and re-layouts: 49.3 us -> 5.24 us
    another operation x6 -> x0, local copies, waits for them, and re-layouts: 37.7 us -> none  [the longest x4 26.9 us: left_gathered(): jnp.stack([padded[offset:offset + tiles] for offset in range(3)], axis=1)]
    slice x4 -> x0, local copies, waits for them, and re-layouts: 16.5 us -> none  [the longest x2 14.8 us: column_product(): extended[:, offset:offset + local_tiles]]
    ppermute x5 -> x0, starting transfers between devices: 14 us -> none  [the longest x2 8.81 us: padded_2(): before = lax.ppermute(last, axis, up)]
    gather x2 -> x0, local copies, waits for them, and re-layouts: 9.05 us -> none  [the longest x1 4.52 us: per_device(): jnp.diagonal(lax.dynamic_slice_in_dim(sigma_odd, start, slab_width, 0))]
  transfers between devices with their start and end apart: 6 -> 0, of which waited for: 5 -> 0; matrix products, arithmetic and copies ran while one was open for 21% -> 0% of each run, Pallas kernels for 0% -> 0%
where the time goes in v1:
time: 165 us; the launch traced here: 164 us
  Pallas kernels  155 us (94%)
  local copies, waits for them, and re-layouts  5.34 us (3%)
  other arithmetic  3.41 us (2%)
    pallas_call x1, Pallas kernels, per_device(): pl.pallas_call(functools.partial(kernel, parts, ranks), out_shape=(jax.Sh...  155 us
    unnamed x4, local copies, waits for them, and re-layouts  5.24 us

profile of v1, /device:TPU:5, one launch (start us, length us, event | category | flops | bytes accessed | tf_op | source)
XLA Modules:
  0.0 164.4 jit_solution(17112192140785435271)
XLA Ops:
  0.6 0.7 convert_element_type.3
  1.3 0.1 copy.6
  1.4 2.7 %broadcast_multiply_fusion.weff_ref = f32[2,4,3,128,128]{4,3,2,1,0:T(8,128)} fusion(f32[2,4,3,128,128]{4,3,2,1,0:T(8,128)} %param.6, f32[2,4,3]{2,1,0:T(4,128)S(1)} %copy.6), kind=kLoop, calls=%fused_computation | loop fusion | flops 393216 | bytes 3145824 | tf_op jit(solution)/shard_map/mul | solution.py:270
  4.1 155.0 %shard_map.59 = (f32[2048,512]{1,0:T(8,128)}, f32[2,512]{1,0:T(2,128)}) custom-call(bf16[2,2048,512]{2,1,0:T(8,128)(2,1)} %local_ref.1, f32[1,2048,512]{2,1,0:T(8,128)} %seed_ref.1, f32[2,4,3,128,128]{4,3,2,1,0:T(8,128)} %broadcast_multiply_fusion.weff_ref), custom_call_target="tpu_custom_call" | custom-call | tf_op jit(solution)/shard_map/pallas_call | solution.py:277
  159.2 0.0 copy-start
  159.2 4.6 %copy.9 = f32[1,2048,512]{2,1,0:T(8,128)} copy(f32[1,2048,512]{2,1,0:T(8,128)} %bitcast.1) | data formatting | bytes 8388608
  163.8 0.0 copy-done
  163.8 0.6 copy.10
Async XLA Ops:
  159.2 4.7 %copy-start = (f32[2,512]{1,0:T(2,128)S(1)}, f32[2,512]{1,0:T(2,128)}, u32[]{:S(2)}) copy-start(f32[2,512]{1,0:T(2,128)} %get-tuple-element.9) | copy-start | bytes 12292

commit v2 on v1

--- a/solution.py
+++ b/solution.py
@@ -25,7 +25,7 @@
     return dot(a_high, b_high) + (dot(a_high, b_low) + dot(a_low, b_high))
 
 
-def kernel(parts, ranks, local_ref, seed_ref, weff_ref, out_ref, var_ref,
+def kernel(parts, ranks, local_ref, seed_ref, band_ref, pattern_ref, out_ref, var_ref,
            nxt, odd, wbuf, m_high, m_low, loc, wc_high, wc_low, wt_high, wt_low,
            wsend, wrecv, nsend, nrecv, hsend, hrecv, lsem):
     p, t = lax.axis_index("tm"), lax.axis_index("tile")
@@ -56,13 +56,6 @@
     def toward(d):
         return (1, has_right) if d == 0 else (-1, has_left)
 
-    def own_w(j, d):
-        step, _ = toward(d)
-        return pltpu.make_async_remote_copy(
-            src_ref=weff_ref.at[j], dst_ref=wbuf.at[j, pl.ds(t * lt, lt)],
-            send_sem=wsend.at[j, d, 0], recv_sem=wrecv.at[j, d, 1],
-            device_id={"tile": t + step}, device_id_type=MESH)
-
     def relay_w(j, d, k):
         step, _ = toward(d)
         part = wbuf.at[j, pl.ds((t - step * k) * lt, lt)]
@@ -86,7 +79,7 @@
         for d in (1, 0):
             @pl.when(toward(d)[1])
             def _(d=d):
-                own_w(j, d).start()
+                relay_w(j, d, 0).start()
 
     def receive(j, k):
         for d in (1, 0):
@@ -98,38 +91,62 @@
                 def _():
                     relay_w(j, d, k).start()
 
-    def seed_copy(index):
+    def block(u):
+        return pl.ds(u * width, width)
+
+    def seed_copy(index, u):
         if index == 0:
             src, dst, target = seed_ref.at[0], nxt.at[:, inner], t
         elif index == 1:
-            src, dst, target = seed_ref.at[0, :, pl.ds(width - tr, tr)], nxt.at[:, left_halo], t + 1
+            src, dst, target = seed_ref.at[0, block(u), pl.ds(width - tr, tr)], nxt.at[block(u), left_halo], t + 1
         else:
-            src, dst, target = seed_ref.at[0, :, pl.ds(0, tr)], nxt.at[:, right_halo], t - 1
+            src, dst, target = seed_ref.at[0, block(u), pl.ds(0, tr)], nxt.at[block(u), right_halo], t - 1
         return pltpu.make_async_remote_copy(
-            src_ref=src, dst_ref=dst, send_sem=nsend.at[index], recv_sem=nrecv.at[index],
+            src_ref=src, dst_ref=dst, send_sem=nsend.at[index, u], recv_sem=nrecv.at[index, u],
             device_id={"tm": p - 1, "tile": target}, device_id_type=MESH)
 
-    seed_sent = ((0, p > 0), (1, (p > 0) & has_right), (2, (p > 0) & has_left))
-    seed_received = ((0, has_next), (1, has_next & has_left), (2, has_next & has_right))
-
-    def halo_copy(d):
+    def halo_copy(d, u):
         if d == 0:
-            src, dst, target = odd.at[:, pl.ds(width, tr)], odd.at[:, left_halo], t + 1
+            src, dst, target = odd.at[block(u), pl.ds(width, tr)], odd.at[block(u), left_halo], t + 1
         else:
-            src, dst, target = odd.at[:, pl.ds(tr, tr)], odd.at[:, right_halo], t - 1
+            src, dst, target = odd.at[block(u), pl.ds(tr, tr)], odd.at[block(u), right_halo], t - 1
         return pltpu.make_async_remote_copy(
-            src_ref=src, dst_ref=dst, send_sem=hsend.at[d], recv_sem=hrecv.at[d],
+            src_ref=src, dst_ref=dst, send_sem=hsend.at[d, u], recv_sem=hrecv.at[d, u],
             device_id={"tile": target}, device_id_type=MESH)
 
-    start_own(1)
-    for index, does in seed_sent:
-        @pl.when(does)
-        def _(index=index):
-            seed_copy(index).start()
-    own_local = [pltpu.make_async_copy(weff_ref.at[j], wbuf.at[j, pl.ds(t * lt, lt)], lsem.at[j]) for j in (0, 1)]
+    def blocks_but(skipped, does, action):
+        @pl.loop(0, ranks)
+        def _(u):
+            @pl.when(does & (u != skipped))
+            def _():
+                action(u)
+
+    def mirror(field):
+        for does, row, place in ((has_left, t * width - tr, left_halo), (has_right, (t + 1) * width, right_halo)):
+            @pl.when(does)
+            def _(row=row, place=place):
+                for i in range(lt):
+                    tile = field[pl.ds(pl.multiple_of(row, tr), tr), pl.ds(tr + i * tr, tr)]
+                    field[pl.ds(pl.multiple_of(t * width + i * tr, tr), tr), place] = tile.T
+
+    own_local = [pltpu.make_async_copy(band_ref.at[j], wbuf.at[j, pl.ds(t * lt, lt)], lsem.at[j]) for j in (0, 1)]
     locals_in = pltpu.make_async_copy(local_ref, loc, lsem.at[2])
-    for copy in own_local + [locals_in]:
+    for copy in own_local[::-1]:
         copy.start()
+    blocks_but(t + 1, (p > 0) & has_right, lambda u: seed_copy(1, u).start())
+    blocks_but(t - 1, (p > 0) & has_left, lambda u: seed_copy(2, u).start())
+
+    @pl.when(p > 0)
+    def _():
+        seed_copy(0, 0).start()
+
+    locals_in.start()
+    for j in (1, 0):
+        own_local[j].wait()
+        for b in range(lt):
+            for k in range(3):
+                at = (j, t * lt + b, k)
+                wbuf[at] = wbuf[at] * pattern_ref[j, b, k].astype(F32)
 
     zero_halo = jnp.zeros((rows, tr), F32)
     for missing, place in ((t == 0, left_halo), (t == ranks - 1, right_halo)):
@@ -150,8 +167,8 @@
         ref[pl.ds(tr + rows, tr), :] = jnp.zeros((tr, width), BF16)
     for ref in (wc_high, wc_low, wt_high, wt_low):
         ref[...] = jnp.zeros_like(ref)
-    for copy in own_local:
-        copy.wait()
+    start_own(1)
+    start_own(0)
 
     chunk = 256
 
@@ -204,11 +221,14 @@
             var_ref[pl.ds(index, 1), pl.ds(c * tr, tr)] = jnp.sum(jnp.where(eye, tile, 0.0), axis=0, keepdims=True)
 
     receive(1, 1)
-    start_own(0)
-    for index, does in seed_received:
-        @pl.when(does)
-        def _(index=index):
-            seed_copy(index).wait_recv()
+
+    @pl.when(has_next)
+    def _():
+        seed_copy(0, 0).wait_recv()
+
+    blocks_but(t, has_next & has_left, lambda u: seed_copy(1, u).wait_recv())
+    blocks_but(t, has_next & has_right, lambda u: seed_copy(2, u).wait_recv())
+    mirror(nxt)
     column_product(nxt, 1)
     locals_in.wait()
     left_rows(1, t, odd, inner)
@@ -220,19 +240,16 @@
         left_round(1, k, odd, inner)
 
     diagonal(1, odd, tr)
-    for d, does in ((1, has_left), (0, has_right)):
-        @pl.when(does)
-        def _(d=d):
-            halo_copy(d).start()
+    mirror(odd)
+    blocks_but(t - 1, has_left, lambda u: halo_copy(1, u).start())
+    blocks_but(t + 1, has_right, lambda u: halo_copy(0, u).start())
 
     @pl.loop(1, ranks - 1)
     def _(k):
         receive(0, k)
 
-    for d, does in ((0, has_left), (1, has_right)):
-        @pl.when(does)
-        def _(d=d):
-            halo_copy(d).wait_recv()
+    blocks_but(t, has_left, lambda u: halo_copy(0, u).wait_recv())
+    blocks_but(t, has_right, lambda u: halo_copy(1, u).wait_recv())
     column_product(odd, 0)
     everything = pl.ds(0, width)
     left_rows(0, t, out_ref, everything)
@@ -249,25 +266,24 @@
         for d in (1, 0):
             @pl.when(toward(d)[1])
             def _(j=j, d=d):
-                own_w(j, d).wait_send()
+                relay_w(j, d, 0).wait_send()
 
                 @pl.loop(1, ranks - 1)
                 def _(k):
                     @pl.when(comes(d, k))
                     def _():
                         relay_w(j, d, k).wait_send()
-    for index, does in seed_sent:
-        @pl.when(does)
-        def _(index=index):
-            seed_copy(index).wait_send()
-    for d, does in ((0, has_right), (1, has_left)):
-        @pl.when(does)
-        def _(d=d):
-            halo_copy(d).wait_send()
+    @pl.when(p > 0)
+    def _():
+        seed_copy(0, 0).wait_send()
+
+    blocks_but(t + 1, (p > 0) & has_right, lambda u: seed_copy(1, u).wait_send())
+    blocks_but(t - 1, (p > 0) & has_left, lambda u: seed_copy(2, u).wait_send())
+    blocks_but(t + 1, has_right, lambda u: halo_copy(0, u).wait_send())
+    blocks_but(t - 1, has_left, lambda u: halo_copy(1, u).wait_send())
 
 
 def per_device(parts, ranks, local_inv, seed_inv, band, pattern):
-    weff = band * pattern.astype(F32)[..., None, None]
     rows, width = seed_inv.shape[1:]
     lt, tr = band.shape[1], band.shape[3]
     tiles = rows // tr
@@ -277,7 +293,7 @@
     out, var = pl.pallas_call(
         functools.partial(kernel, parts, ranks),
         out_shape=(jax.ShapeDtypeStruct((rows, width), F32), jax.ShapeDtypeStruct((2, width), F32)),
-        in_specs=[pl.BlockSpec(memory_space=pl.ANY)] * 3,
+        in_specs=[pl.BlockSpec(memory_space=pltpu.HBM)] * 3 + [pl.BlockSpec(memory_space=pltpu.SMEM)],
         out_specs=(pl.BlockSpec(memory_space=pltpu.VMEM), pl.BlockSpec(memory_space=pltpu.VMEM)),
         scratch_shapes=[
             pltpu.VMEM((rows, width + 2 * tr), F32),
@@ -292,16 +308,16 @@
             pltpu.VMEM((g * tr, span), BF16),
             dma((2, 2, ranks + 1)),
             dma((2, 2, ranks + 1)),
-            dma((3,)),
-            dma((3,)),
-            dma((2,)),
-            dma((2,)),
+            dma((3, ranks)),
+            dma((3, ranks)),
+            dma((2, ranks)),
+            dma((2, ranks)),
             dma((3,)),
         ],
         compiler_params=pltpu.CompilerParams(
-            collective_id=0, has_side_effects=True, vmem_limit_bytes=60 * 1024 * 1024
+            collective_id=0, has_side_effects=True, vmem_limit_bytes=36 * 1024 * 1024
         ),
-    )(local_inv, seed_inv, weff)
+    )(local_inv, seed_inv, band, pattern)
     return out[None], var
 
 

time: 165 us -> 156 us (0.945)
  Pallas kernels: 155 us -> 146 us
  local copies, waits for them, and re-layouts: 5.34 us -> 9.17 us
  other arithmetic: 3.41 us -> 0 us
    pallas_call x1, Pallas kernels: 155 us -> 146 us  [per_device(): pl.pallas_call(functools.partial(kernel, parts, ranks), out_shape=(jax.Sh...]
    unnamed x4 -> x9, local copies, waits for them, and re-layouts: 5.24 us -> 9.17 us
    mul x1 -> x0, other arithmetic: 2.72 us -> none  [per_device(): weff = band * pattern.astype(F32)[..., None, None]]
where the time goes in v2:
time: 156 us
  Pallas kernels  146 us (94%)
  local copies, waits for them, and re-layouts  9.17 us (6%)
    pallas_call x1, Pallas kernels, per_device(): pl.pallas_call(functools.partial(kernel, parts, ranks), out_shape=(jax.Sh...  146 us
    unnamed x9, local copies, waits for them, and re-layouts  9.17 us

profile of v2, /device:TPU:5, one launch (start us, length us, event | category | flops | bytes accessed | tf_op | source)
XLA Modules:
  0.0 155.8 jit_solution(13369687452494590612)
XLA Ops:
  0.6 0.8 copy.6.pattern_ref
  1.4 0.0 copy-start
  1.4 2.2 %copy-done = bf16[2,2048,512]{2,1,0:T(8,128)(2,1)S(1)} copy-done((bf16[2,2048,512]{2,1,0:T(8,128)(2,1)S(1)}, bf16[2,2048,512]{2,1,0:T(8,128)(2,1)}, u32[]{:S(2)}) %copy-start) | copy-done | bytes 4194328
  3.6 0.0 copy-start.1
  3.6 2.2 %copy-done.1 = f32[1,2048,512]{2,1,0:T(8,128)S(1)} copy-done((f32[1,2048,512]{2,1,0:T(8,128)S(1)}, f32[1,2048,512]{2,1,0:T(8,128)}, u32[]{:S(2)}) %copy-start.1) | copy-done | bytes 4194328
  5.8 0.0 copy-start.2
  5.8 1.4 copy-done.2
  7.2 146.0 %shard_map.59 = (f32[2048,512]{1,0:T(8,128)S(1)}, f32[2,512]{1,0:T(2,128)S(1)}) custom-call(bf16[2,2048,512]{2,1,0:T(8,128)(2,1)S(1)} %copy-done, f32[1,2048,512]{2,1,0:T(8,128)S(1)} %copy-done.1, f32[2,4,3,128,128]{4,3,2,1,0:T(8,128)S(1)} %copy-done.2, s32[2,4,3]{2,1,0:T(4,128)S(1)} %copy.6.pattern_ref), custom_call_target="tpu_custom_call" | custom-call | tf_op jit(solution)/shard_map/pallas_call | solution.py:293
  153.2 2.0 %copy.9 = f32[1,2048,512]{2,1,0:T(8,128)} copy(f32[1,2048,512]{2,1,0:T(8,128)S(1)} %bitcast.1) | data formatting | bytes 8388608
  155.2 0.6 copy.10
Async XLA Ops:
  1.4 2.2 %copy-start = (bf16[2,2048,512]{2,1,0:T(8,128)(2,1)S(1)}, bf16[2,2048,512]{2,1,0:T(8,128)(2,1)}, u32[]{:S(2)}) copy-start(bf16[2,2048,512]{2,1,0:T(8,128)(2,1)} %local_ref.1) | copy-start | bytes 12582916
  3.6 2.2 %copy-start.1 = (f32[1,2048,512]{2,1,0:T(8,128)S(1)}, f32[1,2048,512]{2,1,0:T(8,128)}, u32[]{:S(2)}) copy-start(f32[1,2048,512]{2,1,0:T(8,128)} %seed_ref.1) | copy-start | bytes 12582916
  5.8 1.4 copy-start.2

commit v3 on v2

--- a/solution.py
+++ b/solution.py
@@ -30,7 +30,7 @@
            wsend, wrecv, nsend, nrecv, hsend, hrecv, lsem):
     p, t = lax.axis_index("tm"), lax.axis_index("tile")
     rows, width = seed_ref.shape[1], seed_ref.shape[2]
-    tiles, tr = wbuf.shape[1], wbuf.shape[3]
+    tiles, tr = wbuf.shape[1] // 3, wbuf.shape[3]
     lt = width // tr
     g = 2 if lt % 2 == 0 else 1
     span = (g + 2) * tr
@@ -56,21 +56,18 @@
     def toward(d):
         return (1, has_right) if d == 0 else (-1, has_left)
 
-    def relay_w(j, d, k):
+    def with_w(j, d, k, incoming, action):
         step, _ = toward(d)
-        part = wbuf.at[j, pl.ds((t - step * k) * lt, lt)]
-        return pltpu.make_async_remote_copy(
-            src_ref=part, dst_ref=part,
-            send_sem=wsend.at[j, d, k], recv_sem=wrecv.at[j, d, k + 1],
-            device_id={"tile": t + step}, device_id_type=MESH)
-
-    def arriving_w(j, d, k):
-        step, _ = toward(d)
-        part = wbuf.at[j, pl.ds((t - step * k) * lt, lt)]
-        return pltpu.make_async_remote_copy(
-            src_ref=part, dst_ref=part,
-            send_sem=wsend.at[j, d, k], recv_sem=wrecv.at[j, d, k],
-            device_id={"tile": t - step}, device_id_type=MESH)
+        owner = t - step * k
+        at_end = owner == (0 if d == 0 else ranks - 1)
+        for condition, skip in ((at_end, 1), (jnp.logical_not(at_end), 0)):
+            @pl.when(condition)
+            def _(skip=skip):
+                part = wbuf.at[j, pl.ds(owner * lt * 3 + (skip if d == 0 else 0), lt * 3 - skip)]
+                action(pltpu.make_async_remote_copy(
+                    src_ref=part, dst_ref=part,
+                    send_sem=wsend.at[j, d, k], recv_sem=wrecv.at[j, d, k if incoming else k + 1],
+                    device_id={"tile": t - step if incoming else t + step}, device_id_type=MESH))
 
     def comes(d, k):
         return t - k >= 0 if d == 0 else t + k < ranks
@@ -79,17 +76,17 @@
         for d in (1, 0):
             @pl.when(toward(d)[1])
             def _(d=d):
-                relay_w(j, d, 0).start()
+                with_w(j, d, 0, False, lambda copy: copy.start())
 
     def receive(j, k):
         for d in (1, 0):
             @pl.when(comes(d, k))
             def _(d=d):
-                arriving_w(j, d, k).wait_recv()
+                with_w(j, d, k, True, lambda copy: copy.wait_recv())
 
                 @pl.when(toward(d)[1])
                 def _():
-                    relay_w(j, d, k).start()
+                    with_w(j, d, k, False, lambda copy: copy.start())
 
     def block(u):
         return pl.ds(u * width, width)
@@ -129,7 +126,7 @@
                     tile = field[pl.ds(pl.multiple_of(row, tr), tr), pl.ds(tr + i * tr, tr)]
                     field[pl.ds(pl.multiple_of(t * width + i * tr, tr), tr), place] = tile.T
 
-    own_local = [pltpu.make_async_copy(band_ref.at[j], wbuf.at[j, pl.ds(t * lt, lt)], lsem.at[j]) for j in (0, 1)]
+    own_local = [pltpu.make_async_copy(band_ref.at[j], wbuf.at[j, pl.ds(t * lt * 3, lt * 3)], lsem.at[j]) for j in (0, 1)]
     locals_in = pltpu.make_async_copy(local_ref, loc, lsem.at[2])
     for copy in own_local[::-1]:
         copy.start()
@@ -145,8 +142,8 @@
         own_local[j].wait()
         for b in range(lt):
             for k in range(3):
-                at = (j, t * lt + b, k)
-                wbuf[at] = wbuf[at] * pattern_ref[j, b, k].astype(F32)
+                at = (j, (t * lt + b) * 3 + k)
+                wbuf[at] = wbuf[at] * pattern_ref[k, j, b].astype(F32)
 
     zero_halo = jnp.zeros((rows, tr), F32)
     for missing, place in ((t == 0, left_halo), (t == ranks - 1, right_halo)):
@@ -165,6 +162,15 @@
     for ref in (m_high, m_low):
         ref[pl.ds(0, tr), :] = jnp.zeros((tr, width), BF16)
         ref[pl.ds(tr + rows, tr), :] = jnp.zeros((tr, width), BF16)
+    for j in (0, 1):
+        @pl.when(has_left)
+        def _(j=j):
+            wbuf[j, 0] = jnp.zeros((tr, tr), F32)
+
+        @pl.when(has_right)
+        def _(j=j):
+            wbuf[j, tiles * 3 - 1] = jnp.zeros((tr, tr), F32)
+
     for ref in (wc_high, wc_low, wt_high, wt_low):
         ref[...] = jnp.zeros_like(ref)
     start_own(1)
@@ -176,7 +182,7 @@
         for i in range(lt // g):
             for c in range(g):
                 for k in range(3):
-                    high, low = split(wbuf[j, t * lt + i * g + c, k])
+                    high, low = split(wbuf[j, (t * lt + i * g + c) * 3 + k])
                     at = (i, pl.ds((c + k) * tr, tr), pl.ds(c * tr, tr))
                     wc_high[at] = high
                     wc_low[at] = low
@@ -198,7 +204,7 @@
             first = owner * lt + i * g
             for c in range(g):
                 for k in range(3):
-                    high, low = split(wbuf[j, first + c, k].T)
+                    high, low = split(wbuf[j, (first + c) * 3 + k].T)
                     at = (pl.ds(c * tr, tr), pl.ds((c + k) * tr, tr))
                     wt_high[at] = high
                     wt_low[at] = low
@@ -266,13 +272,13 @@
         for d in (1, 0):
             @pl.when(toward(d)[1])
             def _(j=j, d=d):
-                relay_w(j, d, 0).wait_send()
+                with_w(j, d, 0, False, lambda copy: copy.wait_send())
 
                 @pl.loop(1, ranks - 1)
                 def _(k):
                     @pl.when(comes(d, k))
                     def _():
-                        relay_w(j, d, k).wait_send()
+                        with_w(j, d, k, False, lambda copy: copy.wait_send())
     @pl.when(p > 0)
     def _():
         seed_copy(0, 0).wait_send()
@@ -292,13 +298,13 @@
     dma = pltpu.SemaphoreType.DMA
     out, var = pl.pallas_call(
         functools.partial(kernel, parts, ranks),
-        out_shape=(jax.ShapeDtypeStruct((rows, width), F32), jax.ShapeDtypeStruct((2, width), F32)),
+        out_shape=(pltpu.VMEM((rows, width), F32), pltpu.VMEM((2, width), F32)),
         in_specs=[pl.BlockSpec(memory_space=pltpu.HBM)] * 3 + [pl.BlockSpec(memory_space=pltpu.SMEM)],
         out_specs=(pl.BlockSpec(memory_space=pltpu.VMEM), pl.BlockSpec(memory_space=pltpu.VMEM)),
         scratch_shapes=[
             pltpu.VMEM((rows, width + 2 * tr), F32),
             pltpu.VMEM((rows, width + 2 * tr), F32),
-            pltpu.VMEM((2, tiles, 3, tr, tr), F32),
+            pltpu.VMEM((2, tiles * 3, tr, tr), F32),
             pltpu.VMEM((rows + 2 * tr, width), BF16),
             pltpu.VMEM((rows + 2 * tr, width), BF16),
             pltpu.VMEM((2, rows, width), BF16),
@@ -315,9 +321,9 @@
             dma((3,)),
         ],
         compiler_params=pltpu.CompilerParams(
-            collective_id=0, has_side_effects=True, vmem_limit_bytes=36 * 1024 * 1024
+            collective_id=0, has_side_effects=True, vmem_limit_bytes=58 * 1024 * 1024
         ),
-    )(local_inv, seed_inv, band, pattern)
+    )(local_inv, seed_inv, band.reshape(2, lt * 3, tr, tr), pattern.transpose(2, 0, 1))
     return out[None], var
 
 

time: 156 us -> 145 us (0.929)
  local copies, waits for them, and re-layouts: 9.17 us -> 2.61 us
  Pallas kernels: 146 us -> 142 us
    unnamed x9 -> x2, local copies, waits for them, and re-layouts: 9.17 us -> 2.61 us
    pallas_call x1, Pallas kernels: 146 us -> 142 us  [per_device(): pl.pallas_call(functools.partial(kernel, parts, ranks), out_shape=(pltpu....]
where the time goes in v3:
time: 145 us
  Pallas kernels  142 us (98%)
  local copies, waits for them, and re-layouts  2.61 us (2%)
    pallas_call x1, Pallas kernels, per_device(): pl.pallas_call(functools.partial(kernel, parts, ranks), out_shape=(pltpu....  142 us

profile of v3, /device:TPU:5, one launch (start us, length us, event | category | flops | bytes accessed | tf_op | source)
XLA Modules:
  0.0 145.2 jit_solution(5925612976182438473)
XLA Ops:
  0.6 141.9 %shard_map.59 = (f32[2048,512]{1,0:T(8,128)S(1)}, f32[2,512]{1,0:T(2,128)S(1)}) custom-call(bf16[2,2048,512]{2,1,0:T(8,128)(2,1)} %local_ref.1, f32[1,2048,512]{2,1,0:T(8,128)} %seed_ref.1, f32[2,12,128,128]{3,2,1,0:T(8,128)} %bitcast.4, s32[3,2,4]{2,1,0:T(2,128)} %bitcast.5), custom_call_target="tpu_custom_call" | custom-call | tf_op jit(solution)/shard_map/pallas_call | solution.py:299
  142.6 2.0 %copy.8 = f32[1,2048,512]{2,1,0:T(8,128)} copy(f32[1,2048,512]{2,1,0:T(8,128)S(1)} %bitcast.3) | data formatting | bytes 8388608
  144.6 0.6 copy.9

commit v4 on v3

--- a/solution.py
+++ b/solution.py
@@ -227,6 +227,7 @@
             var_ref[pl.ds(index, 1), pl.ds(c * tr, tr)] = jnp.sum(jnp.where(eye, tile, 0.0), axis=0, keepdims=True)
 
     receive(1, 1)
+    receive(0, 1)
 
     @pl.when(has_next)
     def _():
@@ -250,7 +251,7 @@
     blocks_but(t - 1, has_left, lambda u: halo_copy(1, u).start())
     blocks_but(t + 1, has_right, lambda u: halo_copy(0, u).start())
 
-    @pl.loop(1, ranks - 1)
+    @pl.loop(2, ranks - 1)
     def _(k):
         receive(0, k)
 
@@ -264,7 +265,8 @@
     def _(k):
         left_round(0, k, out_ref, everything)
 
-    receive(0, ranks - 1)
+    if ranks > 2:
+        receive(0, ranks - 1)
     left_round(0, ranks - 1, out_ref, everything)
     diagonal(0, out_ref, 0)
 

time: 145 us -> 144 us (level)
  no operation moved by 1% of the time
where the time goes in v4:
time: 144 us
  Pallas kernels  141 us (98%)
  local copies, waits for them, and re-layouts  2.61 us (2%)
    pallas_call x1, Pallas kernels, per_device(): pl.pallas_call(functools.partial(kernel, parts, ranks), out_shape=(pltpu....  141 us

profile of v4, /device:TPU:5, one launch (start us, length us, event | category | flops | bytes accessed | tf_op | source)
XLA Modules:
  0.0 143.8 jit_solution(5923009117954652406)
XLA Ops:
  0.6 140.5 %shard_map.59 = (f32[2048,512]{1,0:T(8,128)S(1)}, f32[2,512]{1,0:T(2,128)S(1)}) custom-call(bf16[2,2048,512]{2,1,0:T(8,128)(2,1)} %local_ref.1, f32[1,2048,512]{2,1,0:T(8,128)} %seed_ref.1, f32[2,12,128,128]{3,2,1,0:T(8,128)} %bitcast.4, s32[3,2,4]{2,1,0:T(2,128)} %bitcast.5), custom_call_target="tpu_custom_call" | custom-call | tf_op jit(solution)/shard_map/pallas_call | solution.py:301
  141.2 2.0 %copy.8 = f32[1,2048,512]{2,1,0:T(8,128)} copy(f32[1,2048,512]{2,1,0:T(8,128)S(1)} %bitcast.3) | data formatting | bytes 8388608
  143.2 0.6 copy.9
